TPU v7x, 128 devices: a whole 4x4x4 slice. The times are simulated.
128 devices in a mesh: group: 8 (over z, core), patch: 16 (over x, y).
Axes of the slice: x: 4, y: 4, z: 4, core: 2. Of those that a mesh axis runs over, the one named last changes fastest.
Arguments:
- node_latent: bfloat16 [40960, 512], P(('group', 'patch')), may hold values from -6 to 6
- fine_latent: bfloat16 [262144, 512], P(('group', 'patch')), may hold values from -6 to 6
- coarse_latent: bfloat16 [65536, 512], P(('group', 'patch')), may hold values from -6 to 6
- fine_sender: int32 [262144], P(('group', 'patch')), may hold values from 0 to 447
- fine_receiver: int32 [262144], P(('group', 'patch')), may hold values from 0 to 319
- coarse_owner: int32 [65536, 1], P(('group', 'patch')), may hold values from 0 to 127; in each aligned block of 512 rows (0 to 511, 512 to 1023, ...) at most 8 rows name the same one
- coarse_row: int32 [65536], P(('group', 'patch')), may hold values from 0 to 15
- coarse_receiver: int32 [65536], P(('group', 'patch')), may hold values from 0 to 15
- edge_first: bfloat16 [2, 1536, 512], replicated, may hold values from -0.15625 to 0.15625
- edge_bias: float32 [2, 512], replicated, may hold values from -3 to 3
- edge_second: bfloat16 [2, 512, 512], replicated, may hold values from -0.25 to 0.25
- edge_gain: float32 [2, 512], replicated, may hold values from 0.25 to 1.75
- node_first: bfloat16 [2, 1024, 512], replicated, may hold values from -0.1875 to 0.1875
- node_bias: float32 [2, 512], replicated, may hold values from -3 to 3
- node_second: bfloat16 [2, 512, 512], replicated, may hold values from -0.25 to 0.25
- node_gain: float32 [2, 512], replicated, may hold values from 0.25 to 1.75
Outputs:
- node_out: bfloat16 [40960, 512], P(('group', 'patch'))
- fine_out: bfloat16 [262144, 512], P(('group', 'patch'))
- coarse_out: bfloat16 [65536, 512], P(('group', 'patch'))
Inputs may be any that keep to these rules, and one draw needn't show every extreme that they name: `fine_sender`: A fine edge's sender indexes the receiving device's patch extended by 64 nodes on each side: values below 64 are the last 64 nodes of the previous patch of the same group, values from 384 on the first 64 nodes of the next patch; patches of a group close into a loop. `coarse_owner`: among the 512 coarse edges of one device, at most 8 have their sender on any one device.
All inputs are finite; a program needn't handle non-finite values.
Results may differ from a plain program's by a relative error of at most 0.0095.
Values may be sent and summed in bfloat16 or wider, within the bound.
A program may use at most 128 MiB of HBM per device.

v0:
```python
import jax
import jax.numpy as jnp
from jax import lax
from jax.sharding import PartitionSpec as P

HALO = 64
COARSE = 16
LAYERS = 2
EPSILON = 1e-05


def padded_2(block, sides, width):
    for axis, dim in sides:
        count = lax.axis_size(axis)
        forward = [(i, i + 1) for i in range(count - 1)]
        forward.append((count - 1, 0))
        backward = [(target, source) for source, target in forward]
        low = lax.ppermute(
            lax.slice_in_dim(block, block.shape[dim] - width, None, axis=dim), axis, forward
        )
        high = lax.ppermute(lax.slice_in_dim(block, 0, width, axis=dim), axis, backward)
        block = jnp.concatenate([low, block, high], axis=dim)
    return block


def norm_rows(values, gain_row):
    centre = jnp.mean(values, axis=-1, keepdims=True)
    centred = values - centre
    variance = jnp.mean(centred * centred, axis=-1, keepdims=True)
    return centred * lax.rsqrt(variance + EPSILON) * gain_row


def select_rows(selector, table):
    return jnp.dot(selector, table, preferred_element_type=jnp.float32).astype(jnp.bfloat16)


def edge_block(latent, endpoints, weight_edge, weight_pair, bias_row, weight_second, gain_row):
    from_ends = jnp.dot(endpoints, weight_pair, preferred_element_type=jnp.float32)
    pre = jnp.dot(latent, weight_edge, preferred_element_type=jnp.float32) + from_ends + bias_row
    hidden = jax.nn.silu(pre).astype(jnp.bfloat16)
    output = jnp.dot(hidden, weight_second, preferred_element_type=jnp.float32)
    message = norm_rows(output, gain_row)
    updated = (latent.astype(jnp.float32) + message).astype(jnp.bfloat16)
    return (updated, message.astype(jnp.bfloat16))


def body(
    node_latent,
    fine_latent,
    coarse_latent,
    fine_sender,
    fine_receiver,
    coarse_owner,
    coarse_row,
    coarse_receiver,
    edge_first,
    edge_bias,
    edge_second,
    edge_gain,
    node_first,
    node_bias,
    node_second,
    node_gain,
):
    width = node_latent.shape[1]
    node_count = node_latent.shape[0]
    devices = lax.axis_size(("group", "patch"))
    halo_rows = HALO
    coarse_nodes = COARSE
    owners = coarse_owner[:, 0]
    gathered_index = owners * coarse_nodes + coarse_row
    node_range = jnp.arange(node_count, dtype=jnp.int32)
    padded_range = jnp.arange(node_count + 2 * halo_rows, dtype=jnp.int32)
    fine_onehot = (node_range[:, None] == fine_receiver[None, :]).astype(jnp.bfloat16)
    coarse_onehot = (node_range[:, None] == coarse_receiver[None, :]).astype(jnp.bfloat16)
    fine_to_receiver = (fine_receiver[:, None] == node_range[None, :]).astype(jnp.bfloat16)
    coarse_to_receiver = (coarse_receiver[:, None] == node_range[None, :]).astype(jnp.bfloat16)
    fine_to_sender = (fine_sender[:, None] == padded_range[None, :]).astype(jnp.bfloat16)
    gathered_range = jnp.arange(devices * coarse_nodes, dtype=jnp.int32)
    coarse_to_sender = (gathered_index[:, None] == gathered_range[None, :]).astype(jnp.bfloat16)
    latent = node_latent
    fine_state = fine_latent
    coarse_state = coarse_latent
    for layer_index in range(LAYERS):
        first = edge_first[layer_index]
        weight_edge = first[:width]
        weight_pair = first[width:]
        bias_row = edge_bias[layer_index]
        weight_second = edge_second[layer_index]
        gain_row = edge_gain[layer_index]
        padded = padded_2(latent, (("patch", 0),), halo_rows)
        own_coarse = latent[:coarse_nodes]
        sender_table = lax.all_gather(own_coarse, ("group", "patch"), axis=0, tiled=True)
        fine_ends = jnp.concatenate(
            [select_rows(fine_to_sender, padded), select_rows(fine_to_receiver, latent)], axis=1
        )
        coarse_ends = jnp.concatenate(
            [select_rows(coarse_to_sender, sender_table), select_rows(coarse_to_receiver, latent)],
            axis=1,
        )
        fine_state, fine_message = edge_block(
            fine_state, fine_ends, weight_edge, weight_pair, bias_row, weight_second, gain_row
        )
        coarse_state, coarse_message = edge_block(
            coarse_state, coarse_ends, weight_edge, weight_pair, bias_row, weight_second, gain_row
        )
        summed = jnp.dot(fine_onehot, fine_message, preferred_element_type=jnp.float32) + jnp.dot(
            coarse_onehot, coarse_message, preferred_element_type=jnp.float32
        )
        summed = summed.astype(jnp.bfloat16)
        node_weights = node_first[layer_index]
        pre = (
            jnp.dot(latent, node_weights[:width], preferred_element_type=jnp.float32)
            + jnp.dot(summed, node_weights[width:], preferred_element_type=jnp.float32)
            + node_bias[layer_index]
        )
        hidden = jax.nn.silu(pre).astype(jnp.bfloat16)
        output = jnp.dot(hidden, node_second[layer_index], preferred_element_type=jnp.float32)
        latent = (latent.astype(jnp.float32) + norm_rows(output, node_gain[layer_index])).astype(
            jnp.bfloat16
        )
    return (latent, fine_state, coarse_state)


def solution(mesh):
    in_specs = (
        P(("group", "patch"), None),
        P(("group", "patch"), None),
        P(("group", "patch"), None),
        P(("group", "patch")),
        P(("group", "patch")),
        P(("group", "patch"), None),
        P(("group", "patch")),
        P(("group", "patch")),
        P(),
        P(),
        P(),
        P(),
        P(),
        P(),
        P(),
        P(),
    )
    out_specs = (
        P(("group", "patch"), None),
        P(("group", "patch"), None),
        P(("group", "patch"), None),
    )
    return jax.shard_map(body, mesh=mesh, in_specs=in_specs, out_specs=out_specs, check_vma=False)
```

profile of v0, /device:TPU:1, one launch (start us, length us, event | category | flops | bytes accessed | tf_op | source)
XLA Modules:
  0.0 181.6 jit_solution(11054618840922823359)
XLA Ops:
  9.6 2.2 %collective-permute-start = (bf16[64,512]{1,0:T(8,128)(2,1)S(1)}, bf16[64,512]{1,0:T(8,128)(2,1)S(1)}, u32[]{:S(2)}, u32[]{:S(2)}) collective-permute-start(bf16[64,512]{1,0:T(8,128)(2,1)S(1)} %get-tuple-element.8), channel_id=1, source_target_pairs={{0,1},{1,2},{2,3},{3,4},{4,5},{5,6},{6,7},{7,8},{8,9},{9,10},{10,1... | collective-permute-start | bytes 196616 | tf_op jit(solution)/shard_map/ppermute | solution.py:18
  11.8 3.7 %collective-permute-start.1 = (bf16[64,512]{1,0:T(8,128)(2,1)S(1)}, bf16[64,512]{1,0:T(8,128)(2,1)S(1)}, u32[]{:S(2)}, u32[]{:S(2)}) collective-permute-start(bf16[64,512]{1,0:T(8,128)(2,1)S(1)} %get-tuple-element.9), channel_id=1, source_target_pairs={{1,0},{2,1},{3,2},{4,3},{5,4},{6,5},{7,6},{8,7},{9,8},{10,9},{11,1... | collective-permute-start | bytes 196616 | tf_op jit(solution)/shard_map/ppermute | solution.py:21
  17.8 2.3 %convolution_convert_fusion.1 = bf16[512,512]{1,0:T(8,128)(2,1)} fusion(bf16[320,512]{1,0:T(8,128)(2,1)} %param.16, s32[512]{0:T(512)} %param.23), kind=kOutput, calls=%fused_computation.55 | convolution fusion | flops 168198144 | bytes 854016 | tf_op jit(solution)/shard_map/dot_general | solution.py:34
  20.0 2.3 %fusion.106 = f32[320,512]{1,0:T(8,128)} fusion(bf16[320,512]{1,0:T(8,128)(2,1)} %param.16, bf16[2,1024,512]{2,1,0:T(8,128)(2,1)} %param.28), kind=kOutput, calls=%fused_computation.118 | convolution fusion | flops 167772160 | bytes 1507328 | tf_op jit(solution)/shard_map/dot_general | solution.py:113
  22.4 2.7 %fusion.102 = f32[512,512]{1,0:T(8,128)} fusion(bf16[512,512]{1,0:T(8,128)(2,1)} %param.18, bf16[2,1536,512]{2,1,0:T(8,128)(2,1)} %param.24), kind=kOutput, calls=%fused_computation.115 | convolution fusion | flops 268435456 | bytes 2097152 | tf_op jit(solution)/shard_map/dot_general | solution.py:39
  25.2 2.5 %fusion.18 = bf16[2048,512]{1,0:T(8,128)(2,1)} fusion(bf16[320,512]{1,0:T(8,128)(2,1)S(1)} %copy-done.7, s32[2048]{0:T(1024)S(1)} %copy-done.15), kind=kOutput, calls=%fused_computation.29 | convolution fusion | flops 672792576 | bytes 2433024 | tf_op jit(solution)/shard_map/dot_general | solution.py:34
  28.7 2.4 %copy.19 = bf16[2048,512]{0,1:T(8,128)(2,1)} copy(bf16[2048,512]{1,0:T(8,128)(2,1)S(1)} %copy-done.5) | data formatting | bytes 4194304 | tf_op args[1]
  31.2 1.7 fusion.16
  33.0 5.6 %fusion = f32[2048,512]{1,0:T(8,128)} fusion(bf16[2048,512]{1,0:T(8,128)(2,1)S(1)} %copy-done.19, bf16[2048,512]{1,0:T(8,128)(2,1)S(1)} %fusion.16, bf16[2,1536,512]{2,1,0:T(8,128)(2,1)} %param.24), kind=kOutput, calls=%fused_computation | convolution fusion | flops 2155872256 | bytes 9437184 | tf_op jit(solution)/shard_map/dot_general | solution.py:38
  38.6 7.1 %fusion.174 = (f32[2048]{0:T(1024)S(1)}, f32[2048,512]{0,1:T(8,128)}) fusion(bf16[2,512,512]{2,1,0:T(8,128)(2,1)S(1)} %copy-done.13, f32[2048,512]{1,0:T(8,128)} %fusion, bf16[2048,512]{1,0:T(8,128)(2,1)S(1)} %copy-done.5, f32[512]{0:T(512)S(1)} %bitcast.116, bf16[2,1536,512]{2,1,0:T(8,128)(2,1)} %param.24), kind=kOutput, calls=%fused_computation.187 | convolution fusion | flops 2155870208 | bytes 11544576 | tf_op jit(solution)/shard_map/dot_general | solution.py:41
  45.7 2.8 %multiply_reduce_fusion.1 = f32[2048]{0:T(1024)S(1)} fusion(f32[2048,512]{0,1:T(8,128)} %get-tuple-element.19, f32[2048]{0:T(1024)S(1)} %broadcast_multiply_fusion.1), kind=kLoop, calls=%fused_computation.17 | loop fusion | flops 3143680 | bytes 4210688 | tf_op jit(solution)/shard_map/reduce_sum | solution.py:29
  49.1 2.0 %fusion.21 = f32[320,512]{1,0:T(8,128)} fusion(f32[2048,512]{0,1:T(8,128)S(1)} %copy-done.1, f32[512]{0:T(512)S(1)} %bitcast.105, f32[2048]{0:T(1024)S(1)} %add_rsqrt_fusion.1, f32[2048]{0:T(1024)S(1)} %broadcast_multiply_fusion.1, s32[2048]{0:T(1024)S(1)} %copy-done.15), kind=kOutput, calls=%fused_computation.33 | convolution fusion | flops 675938304 | bytes 4876288 | tf_op jit(solution)/shard_map/dot_general | solution.py:107
  52.3 28.3 %all-gather.3.cloned.1.call-done = bf16[2048,512]{1,0:T(8,128)(2,1)} async-done(((bf16[16,512]{1,0:T(8,128)(2,1)}), bf16[2048,512]{1,0:T(8,128)(2,1)}) %all-gather.3.cloned.1.call-update) | async-done | bytes 2097168 | tf_op jit(solution)/shard_map/all_gather | solution.py:93
  80.6 3.7 %fusion.42 = bf16[512,512]{1,0:T(8,128)(2,1)} fusion(bf16[2048,512]{1,0:T(8,128)(2,1)} %all-gather.3.cloned.1.call-done, s32[512]{0:T(512)S(1)} %add.176), kind=kOutput, calls=%fused_computation.56 | convolution fusion | flops 1075052544 | bytes 2623488 | tf_op jit(solution)/shard_map/dot_general | solution.py:34
  84.3 3.3 %fusion.177 = (f32[512]{0:T(512)S(1)}, f32[512,512]{0,1:T(8,128)S(1)}) fusion(bf16[2,512,512]{2,1,0:T(8,128)(2,1)} %param.26, f32[512,512]{1,0:T(8,128)} %fusion.102, bf16[2,1536,512]{2,1,0:T(8,128)(2,1)} %param.24, bf16[512,512]{1,0:T(8,128)(2,1)} %convolution_convert_fusion.1, bf16[512,512]{1,0:T(8,128)(2,1)} %fusion.42, f32[512]{0:T(512)S(1)} %bitcast.117), kind=kOutput, calls=%fused_computation.188 | convolution fusion | flops 809500160 | bytes 4722688 | tf_op jit(solution)/shard_map/dot_general | solution.py:41
  87.8 2.4 %multiply_convert_fusion.5 = bf16[320,512]{1,0:T(8,128)(2,1)S(1)} fusion(f32[320,512]{1,0:T(8,128)} %fusion.106, f32[320,512]{1,0:T(8,128)} %fusion.21, f32[512,512]{0,1:T(8,128)S(1)} %get-tuple-element.21, bf16[2,1024,512]{2,1,0:T(8,128)(2,1)} %param.28, f32[512]{0:T(512)S(1)} %bitcast.107, f32[512]{0:T(512)S(1)} %add_rsqrt_fusion.5, ...), kind=kOutput, calls=%fused_computation.98 | convolution fusion | flops 338231296 | bytes 3221504 | tf_op jit(solution)/shard_map/dot_general | solution.py:114
  90.2 1.5 fusion.182
  93.7 2.5 %fusion.19 = bf16[2048,512]{1,0:T(8,128)(2,1)} fusion(bf16[320,512]{1,0:T(8,128)(2,1)S(1)} %add_convert_fusion.5, s32[2048]{0:T(1024)S(1)} %copy-done.15), kind=kOutput, calls=%fused_computation.30 | convolution fusion | flops 672792576 | bytes 2433024 | tf_op jit(solution)/shard_map/dot_general | solution.py:34
  97.5 2.5 %fusion.91 = f32[512,512]{1,0:T(8,128)} fusion(bf16[512,512]{0,1:T(8,128)(2,1)S(1)} %add_convert_fusion.3, bf16[2,1536,512]{2,1,0:T(8,128)(2,1)} %param.24), kind=kOutput, calls=%fused_computation.105 | convolution fusion | flops 268435456 | bytes 2097152 | tf_op jit(solution)/shard_map/dot_general | solution.py:39
  100.3 4.8 %collective-permute-start.3 = (bf16[64,512]{1,0:T(8,128)(2,1)S(1)}, bf16[64,512]{1,0:T(8,128)(2,1)S(1)}, u32[]{:S(2)}, u32[]{:S(2)}) collective-permute-start(bf16[64,512]{1,0:T(8,128)(2,1)S(1)} %get-tuple-element.7), channel_id=1, source_target_pairs={{1,0},{2,1},{3,2},{4,3},{5,4},{6,5},{7,6},{8,7},{9,8},{10,9},{11,1... | collective-permute-start | bytes 196616 | tf_op jit(solution)/shard_map/ppermute | solution.py:21
  105.1 2.2 %fusion.95 = f32[320,512]{1,0:T(8,128)} fusion(bf16[320,512]{1,0:T(8,128)(2,1)S(1)} %add_convert_fusion.5, bf16[2,1024,512]{2,1,0:T(8,128)(2,1)} %param.28), kind=kOutput, calls=%fused_computation.108 | convolution fusion | flops 167772160 | bytes 1507328 | tf_op jit(solution)/shard_map/dot_general | solution.py:113
  108.6 1.5 fusion.17
  110.2 5.5 %fusion.4 = f32[2048,512]{1,0:T(8,128)} fusion(bf16[2048,512]{1,0:T(8,128)(2,1)S(1)} %copy-done.18, bf16[2048,512]{1,0:T(8,128)(2,1)S(1)} %fusion.17, bf16[2,1536,512]{2,1,0:T(8,128)(2,1)} %param.24), kind=kOutput, calls=%fused_computation.4 | convolution fusion | flops 2155872256 | bytes 9437184 | tf_op jit(solution)/shard_map/dot_general | solution.py:38
  115.7 7.4 %fusion.183 = (f32[2048]{0:T(1024)S(1)}, f32[2048,512]{0,1:T(8,128)}) fusion(bf16[2,512,512]{2,1,0:T(8,128)(2,1)} %param.26, f32[2048,512]{1,0:T(8,128)} %fusion.4, bf16[2048,512]{0,1:T(8,128)(2,1)S(1)} %add_convert_fusion.1, f32[512]{0:T(512)S(1)} %bitcast.113, bf16[2,1536,512]{2,1,0:T(8,128)(2,1)} %param.24), kind=kOutput, calls=%fused_computation.190 | convolution fusion | flops 2155870208 | bytes 11544576 | tf_op jit(solution)/shard_map/dot_general | solution.py:41
  123.1 2.8 %multiply_reduce_fusion = f32[2048]{0:T(1024)S(1)} fusion(f32[2048,512]{0,1:T(8,128)} %get-tuple-element.25, f32[2048]{0:T(1024)S(1)} %broadcast_multiply_fusion), kind=kLoop, calls=%fused_computation.10 | loop fusion | flops 3143680 | bytes 4210688 | tf_op jit(solution)/shard_map/reduce_sum | solution.py:29
  126.5 2.4 %add_convert_fusion = bf16[2048,512]{0,1:T(8,128)(2,1)} fusion(bf16[2048,512]{0,1:T(8,128)(2,1)S(1)} %add_convert_fusion.1, f32[2048,512]{0,1:T(8,128)S(1)} %copy-done, f32[512]{0:T(512)S(1)} %bitcast.101, f32[2048]{0:T(1024)S(1)} %add_rsqrt_fusion, f32[2048]{0:T(1024)S(1)} %broadcast_multiply_fusion), kind=kLoop, calls=%fused_computation.8 | loop fusion | flops 6291456 | bytes 8407040 | tf_op jit(solution)/shard_map/convert_element_type | solution.py:43
  128.9 3.9 %copy.21 = bf16[2048,512]{1,0:T(8,128)(2,1)} copy(bf16[2048,512]{0,1:T(8,128)(2,1)} %add_convert_fusion) | data formatting | bytes 4194304
  132.9 4.1 %fusion.20 = f32[320,512]{1,0:T(8,128)} fusion(f32[2048,512]{0,1:T(8,128)} %get-tuple-element.25, f32[512]{0:T(512)S(1)} %bitcast.102, f32[2048]{0:T(1024)S(1)} %add_rsqrt_fusion, f32[2048]{0:T(1024)S(1)} %broadcast_multiply_fusion, s32[2048]{0:T(1024)S(1)} %copy-done.15), kind=kOutput, calls=%fused_computation.32 | convolution fusion | flops 675938304 | bytes 4876288 | tf_op jit(solution)/shard_map/dot_general | solution.py:107
  137.0 25.9 %all-gather.5.cloned.1.call-done = bf16[2048,512]{1,0:T(8,128)(2,1)} async-done(((bf16[16,512]{1,0:T(8,128)(2,1)}), bf16[2048,512]{1,0:T(8,128)(2,1)}) %all-gather.5.cloned.1.call-update) | async-done | bytes 2097168 | tf_op jit(solution)/shard_map/all_gather | solution.py:93
  163.0 3.7 %fusion.43 = bf16[512,512]{1,0:T(8,128)(2,1)} fusion(bf16[2048,512]{1,0:T(8,128)(2,1)} %all-gather.5.cloned.1.call-done, s32[512]{0:T(512)S(1)} %add.176), kind=kOutput, calls=%fused_computation.57 | convolution fusion | flops 1075052544 | bytes 2623488 | tf_op jit(solution)/shard_map/dot_general | solution.py:34
  166.6 2.8 %fusion.186 = (f32[512]{0:T(512)S(1)}, f32[512,512]{0,1:T(8,128)S(1)}) fusion(bf16[2,512,512]{2,1,0:T(8,128)(2,1)} %param.26, f32[512,512]{1,0:T(8,128)S(1)} %copy-done.9, bf16[2,1536,512]{2,1,0:T(8,128)(2,1)} %param.24, bf16[512,512]{1,0:T(8,128)(2,1)S(1)} %copy-done.17, bf16[512,512]{1,0:T(8,128)(2,1)} %fusion.43, f32[512]{0:T(512)S(1)} %bitcast.114), kind=kOutput, calls=%fused_computation.191 | convolution fusion | flops 809500160 | bytes 4722688 | tf_op jit(solution)/shard_map/dot_general | solution.py:41
  170.9 2.2 %multiply_convert_fusion.4 = bf16[320,512]{1,0:T(8,128)(2,1)S(1)} fusion(f32[320,512]{1,0:T(8,128)} %fusion.95, f32[320,512]{1,0:T(8,128)} %fusion.20, f32[512,512]{0,1:T(8,128)S(1)} %get-tuple-element.27, bf16[2,1024,512]{2,1,0:T(8,128)(2,1)} %param.28, f32[512]{0:T(512)S(1)} %bitcast.104, f32[512]{0:T(512)S(1)} %add_rsqrt_fusion.3, ...), kind=kOutput, calls=%fused_computation.95 | convolution fusion | flops 338231296 | bytes 3221504 | tf_op jit(solution)/shard_map/dot_general | solution.py:114
  (84 shorter events, 16.3 us)
Async XLA Ops:
  7.2 18.0 %copy-start.7 = (bf16[320,512]{1,0:T(8,128)(2,1)S(1)}, bf16[320,512]{1,0:T(8,128)(2,1)}, u32[]{:S(2)}) copy-start(bf16[320,512]{1,0:T(8,128)(2,1)} %param.16) | copy-start | bytes 983044
  7.2 17.9 %copy-start.10 = (f32[2,512]{1,0:T(2,128)S(1)}, f32[2,512]{1,0:T(2,128)}, u32[]{:S(2)}) copy-start(f32[2,512]{1,0:T(2,128)} %param.31) | copy-start | bytes 12292
  7.2 18.0 %copy-start.15 = (s32[2048]{0:T(1024)S(1)}, s32[2048]{0:T(1024)}, u32[]{:S(2)}) copy-start(s32[2048]{0:T(1024)} %param.20) | copy-start | bytes 24580
  7.2 73.4 %all-gather.3.cloned.1.call-start = ((), (), s32[]{:S(2)}) async-start(), calls=%async_computation | async-start | bytes 2113536 | tf_op jit(solution)/shard_map/all_gather | solution.py:93
  8.6 154.3 %all-gather.5.cloned.1.call-start = ((), (), s32[]{:S(2)}) async-start(), calls=%async_computation.1 | async-start | bytes 2113536 | tf_op jit(solution)/shard_map/all_gather | solution.py:93
  9.6 21.6 %collective-permute-start = (bf16[64,512]{1,0:T(8,128)(2,1)S(1)}, bf16[64,512]{1,0:T(8,128)(2,1)S(1)}, u32[]{:S(2)}, u32[]{:S(2)}) collective-permute-start(bf16[64,512]{1,0:T(8,128)(2,1)S(1)} %get-tuple-element.8), channel_id=1, source_target_pairs={{0,1},{1,2},{2,3},{3,4},{4,5},{5,6},{6,7},{7,8},{8,9},{9,10},{10,1... | collective-permute-start | bytes 196616 | tf_op jit(solution)/shard_map/ppermute | solution.py:18
  11.8 19.4 %collective-permute-start.1 = (bf16[64,512]{1,0:T(8,128)(2,1)S(1)}, bf16[64,512]{1,0:T(8,128)(2,1)S(1)}, u32[]{:S(2)}, u32[]{:S(2)}) collective-permute-start(bf16[64,512]{1,0:T(8,128)(2,1)S(1)} %get-tuple-element.9), channel_id=1, source_target_pairs={{1,0},{2,1},{3,2},{4,3},{5,4},{6,5},{7,6},{8,7},{9,8},{10,9},{11,1... | collective-permute-start | bytes 196616 | tf_op jit(solution)/shard_map/ppermute | solution.py:21
  22.4 5.3 %copy-start.12 = (s32[512,1]{0,1:T(1,128)S(1)}, s32[512,1]{0,1:T(1,128)}, u32[]{:S(2)}) copy-start(s32[512,1]{0,1:T(1,128)} %param.21) | copy-start | bytes 6148
  22.4 5.3 %copy-start.6 = (bf16[512,512]{1,0:T(8,128)(2,1)S(1)}, bf16[512,512]{1,0:T(8,128)(2,1)}, u32[]{:S(2)}) copy-start(bf16[512,512]{1,0:T(8,128)(2,1)} %param.18) | copy-start | bytes 1572868
  25.1 3.6 %copy-start.5 = (bf16[2048,512]{1,0:T(8,128)(2,1)S(1)}, bf16[2048,512]{1,0:T(8,128)(2,1)}, u32[]{:S(2)}) copy-start(bf16[2048,512]{1,0:T(8,128)(2,1)} %param.17) | copy-start | bytes 6291460
  27.7 3.5 %copy-start.11 = (s32[512]{0:T(512)S(1)}, s32[512]{0:T(512)}, u32[]{:S(2)}) copy-start(s32[512]{0:T(512)} %param.22) | copy-start | bytes 6148
  27.7 3.5 %copy-start.14 = (s32[2048]{0:T(1024)S(1)}, s32[2048]{0:T(1024)}, u32[]{:S(2)}) copy-start(s32[2048]{0:T(1024)} %param.19) | copy-start | bytes 24580
  31.1 1.8 copy-start.19
  32.9 5.6 %copy-start.13 = (bf16[2,512,512]{2,1,0:T(8,128)(2,1)S(1)}, bf16[2,512,512]{2,1,0:T(8,128)(2,1)}, u32[]{:S(2)}) copy-start(bf16[2,512,512]{2,1,0:T(8,128)(2,1)} %param.26) | copy-start | bytes 3145732
  45.7 3.4 %copy-start.1 = (f32[2048,512]{0,1:T(8,128)S(1)}, f32[2048,512]{0,1:T(8,128)}, u32[]{:S(2)}) copy-start(f32[2048,512]{0,1:T(8,128)} %get-tuple-element.19) | copy-start | bytes 12582916
  48.5 2.6 %copy-start.2 = (bf16[2048,512]{0,1:T(8,128)(2,1)S(1)}, bf16[2048,512]{0,1:T(8,128)(2,1)}, u32[]{:S(2)}) copy-start(bf16[2048,512]{0,1:T(8,128)(2,1)} %copy.19) | copy-start | bytes 6291460
  84.3 3.5 %copy-start.16 = (s32[512]{0:T(512)S(1)}, s32[512]{0:T(512)}, u32[]{:S(2)}) copy-start(s32[512]{0:T(512)} %param.23) | copy-start | bytes 6148
  87.6 4.3 %copy-start.3 = (f32[512,512]{0,1:T(8,128)}, f32[512,512]{0,1:T(8,128)S(1)}, u32[]{:S(2)}) copy-start(f32[512,512]{0,1:T(8,128)S(1)} %get-tuple-element.21) | copy-start | bytes 3145732
  93.7 2.5 %copy-start.4 = (f32[512,512]{0,1:T(8,128)S(1)}, f32[512,512]{0,1:T(8,128)}, u32[]{:S(2)}) copy-start(f32[512,512]{0,1:T(8,128)} %copy-done.3) | copy-start | bytes 3145732
  100.0 8.6 %collective-permute-start.2 = (bf16[64,512]{1,0:T(8,128)(2,1)S(1)}, bf16[64,512]{1,0:T(8,128)(2,1)S(1)}, u32[]{:S(2)}, u32[]{:S(2)}) collective-permute-start(bf16[64,512]{1,0:T(8,128)(2,1)S(1)} %get-tuple-element.6), channel_id=1, source_target_pairs={{0,1},{1,2},{2,3},{3,4},{4,5},{5,6},{6,7},{7,8},{8,9},{9,10},{10,1... | collective-permute-start | bytes 196616 | tf_op jit(solution)/shard_map/ppermute | solution.py:18
  100.3 8.3 %collective-permute-start.3 = (bf16[64,512]{1,0:T(8,128)(2,1)S(1)}, bf16[64,512]{1,0:T(8,128)(2,1)S(1)}, u32[]{:S(2)}, u32[]{:S(2)}) collective-permute-start(bf16[64,512]{1,0:T(8,128)(2,1)S(1)} %get-tuple-element.7), channel_id=1, source_target_pairs={{1,0},{2,1},{3,2},{4,3},{5,4},{6,5},{7,6},{8,7},{9,8},{10,9},{11,1... | collective-permute-start | bytes 196616 | tf_op jit(solution)/shard_map/ppermute | solution.py:21
  107.3 2.8 %copy-start.18 = (bf16[2048,512]{1,0:T(8,128)(2,1)S(1)}, bf16[2048,512]{1,0:T(8,128)(2,1)}, u32[]{:S(2)}) copy-start(bf16[2048,512]{1,0:T(8,128)(2,1)} %fusion.19) | copy-start | bytes 6291460
  123.1 3.4 %copy-start = (f32[2048,512]{0,1:T(8,128)S(1)}, f32[2048,512]{0,1:T(8,128)}, u32[]{:S(2)}) copy-start(f32[2048,512]{0,1:T(8,128)} %get-tuple-element.25) | copy-start | bytes 12582916
  137.0 29.6 %copy-start.9 = (f32[512,512]{1,0:T(8,128)S(1)}, f32[512,512]{1,0:T(8,128)}, u32[]{:S(2)}) copy-start(f32[512,512]{1,0:T(8,128)} %fusion.91) | copy-start | bytes 3145732
  137.0 29.6 %copy-start.17 = (bf16[512,512]{1,0:T(8,128)(2,1)S(1)}, bf16[512,512]{1,0:T(8,128)(2,1)}, u32[]{:S(2)}) copy-start(bf16[512,512]{1,0:T(8,128)(2,1)} %convolution_convert_fusion) | copy-start | bytes 1572868
  169.9 3.2 %copy-start.8 = (bf16[2,512,512]{2,1,0:T(8,128)(2,1)S(1)}, bf16[2,512,512]{2,1,0:T(8,128)(2,1)}, u32[]{:S(2)}) copy-start(bf16[2,512,512]{2,1,0:T(8,128)(2,1)} %param.30) | copy-start | bytes 3145732
Sparse Core Ops, SparseCore 0:
  11.6 68.9 all-gather.2
  100.1 62.7 all-gather.4
where the time goes:
time: 182 us
  matrix products  73.3 us (40%)
  waiting for transfers between devices  54.3 us (30%)
  local copies, waits for them, and re-layouts  14.9 us (8%)
  between operations  14.3 us (8%)
  other arithmetic  13.7 us (8%)
  starting transfers between devices  11 us (6%)
    all_gather x2, waiting for transfers between devices, body(): lax.all_gather(own_coarse, ('group', 'patch'), axis=0, tiled=True)  54.3 us
    dot_general x4, matrix products, edge_block(): output = jnp.dot(hidden, weight_second, preferred_element_type=jnp.float32)  20.6 us
    dot_general x8, matrix products, select_rows(): jnp.dot(selector, table, preferred_element_type=jnp.float32)  19.2 us
    dot_general x2, matrix products, edge_block(): jnp.dot(endpoints, weight_pair, preferred_element_type=jnp.float32)  11.1 us
    unnamed x44, local copies, waits for them, and re-layouts  9.72 us
    ppermute x2, starting transfers between devices, padded_2(): lax.ppermute(lax.slice_in_dim(block, 0, width, axis=dim), axis, backward)  8.49 us
    reduce_sum x6, other arithmetic, norm_rows(): variance = jnp.mean(centred * centred, axis=-1, keepdims=True)  6.42 us
    dot_general x2, matrix products, body(): jnp.dot(fine_onehot, fine_message, preferred_element_type=jnp.float32)  6.12 us
  transfers between devices with their start and end apart: 6, of which 2 were waited for; matrix products, arithmetic and copies ran while one was open for 38% of the time, Pallas kernels for 0%

commit v1 on v0

--- a/solution.py
+++ b/solution.py
@@ -90,7 +90,15 @@
         gain_row = edge_gain[layer_index]
         padded = padded_2(latent, (("patch", 0),), halo_rows)
         own_coarse = latent[:coarse_nodes]
-        sender_table = lax.all_gather(own_coarse, ("group", "patch"), axis=0, tiled=True)
+        sender_table = jnp.concatenate(
+            lax.all_to_all(
+                jnp.stack([own_coarse] * lax.axis_size(("group", "patch"))),
+                ("group", "patch"),
+                0,
+                0,
+            ),
+            axis=0,
+        )
         fine_ends = jnp.concatenate(
             [select_rows(fine_to_sender, padded), select_rows(fine_to_receiver, latent)], axis=1
         )

time: 182 us -> 129 us (0.71)
  waiting for transfers between devices: 54.3 us -> 0.94 us
  starting transfers between devices: 11 us -> 26.3 us
  between operations: 14.3 us -> 1.04 us
  other arithmetic: 13.7 us -> 11.7 us
    all_gather x2 -> x0, waiting for transfers between devices: 54.3 us -> none  [body(): lax.all_gather(own_coarse, ('group', 'patch'), axis=0, tiled=True)]
    all_to_all x0 -> x2, starting transfers between devices: none -> 15.6 us  [body(): lax.all_to_all(jnp.stack([own_coarse] * lax.axis_size(('group', 'patch'))...]
    another operation x0 -> x2, local copies, waits for them, and re-layouts: none -> 3.18 us  [body(): jnp.stack([own_coarse] * lax.axis_size(('group', 'patch')))]
    unnamed x44 -> x50, local copies, waits for them, and re-layouts: 9.72 us -> 9.76 us
  transfers between devices with their start and end apart: 6 -> 6, of which waited for: 2 -> 1; matrix products, arithmetic and copies ran while one was open for 38% -> 51% of each run, Pallas kernels for 0% -> 0%
where the time goes in v1:
time: 129 us; the launch traced here: 128 us
  matrix products  73.1 us (57%)
  starting transfers between devices  26.3 us (20%)
  local copies, waits for them, and re-layouts  14.7 us (11%)
  other arithmetic  11.7 us (9%)
    dot_general x4, matrix products, edge_block(): output = jnp.dot(hidden, weight_second, preferred_element_type=jnp.float32)  20.7 us
    dot_general x8, matrix products, select_rows(): jnp.dot(selector, table, preferred_element_type=jnp.float32)  18.3 us
    all_to_all x2, starting transfers between devices, body(): lax.all_to_all(jnp.stack([own_coarse] * lax.axis_size(('group', 'patch'))...  15.6 us
    dot_general x2, matrix products, edge_block(): jnp.dot(endpoints, weight_pair, preferred_element_type=jnp.float32)  11.1 us
    unnamed x50, local copies, waits for them, and re-layouts  9.76 us
    ppermute x2, starting transfers between devices, padded_2(): lax.ppermute(lax.slice_in_dim(block, 0, width, axis=dim), axis, backward)  7.15 us
    reduce_sum x6, other arithmetic, norm_rows(): variance = jnp.mean(centred * centred, axis=-1, keepdims=True)  6.42 us
    dot_general x2, matrix products, body(): jnp.dot(fine_onehot, fine_message, preferred_element_type=jnp.float32)  6.11 us
  transfers between devices with their start and end apart: 6, of which 1 were waited for; matrix products, arithmetic and copies ran while one was open for 51% of the time, Pallas kernels for 0%

profile of v1, /device:TPU:1, one launch (start us, length us, event | category | flops | bytes accessed | tf_op | source)
XLA Modules:
  0.0 127.7 jit_solution(3328317710258392440)
XLA Ops:
  1.7 2.2 %collective-permute-start = (bf16[64,512]{1,0:T(8,128)(2,1)S(1)}, bf16[64,512]{1,0:T(8,128)(2,1)S(1)}, u32[]{:S(2)}, u32[]{:S(2)}) collective-permute-start(bf16[64,512]{1,0:T(8,128)(2,1)S(1)} %get-tuple-element.8), channel_id=1, source_target_pairs={{0,1},{1,2},{2,3},{3,4},{4,5},{5,6},{6,7},{7,8},{8,9},{9,10},{10,1... | collective-permute-start | bytes 196616 | tf_op jit(solution)/shard_map/ppermute | solution.py:18
  3.9 3.7 %collective-permute-start.1 = (bf16[64,512]{1,0:T(8,128)(2,1)S(1)}, bf16[64,512]{1,0:T(8,128)(2,1)S(1)}, u32[]{:S(2)}, u32[]{:S(2)}) collective-permute-start(bf16[64,512]{1,0:T(8,128)(2,1)S(1)} %get-tuple-element.9), channel_id=1, source_target_pairs={{1,0},{2,1},{3,2},{4,3},{5,4},{6,5},{7,6},{8,7},{9,8},{10,9},{11,1... | collective-permute-start | bytes 196616 | tf_op jit(solution)/shard_map/ppermute | solution.py:21
  8.3 1.6 %stack.4 = bf16[128,16,512]{2,1,0:T(8,128)(2,1)} broadcast(bf16[16,512]{1,0:T(8,128)(2,1)S(1)} %slice.125), dimensions={1,2} | broadcast | bytes 2113536 | tf_op jit(solution)/shard_map/stack | solution.py:95
  9.9 8.1 %all-to-all-start = ((bf16[128,16,512]{2,1,0:T(8,128)(2,1)}), bf16[128,16,512]{2,1,0:T(8,128)(2,1)}, u32[]{:S(2)}, u32[]{:S(2)}) async-start(bf16[128,16,512]{2,1,0:T(8,128)(2,1)} %stack.4), calls=%async_computation | async-start | bytes 4194304 | tf_op jit(solution)/shard_map/all_to_all | solution.py:94
  19.4 2.3 %fusion.106 = f32[320,512]{1,0:T(8,128)} fusion(bf16[320,512]{1,0:T(8,128)(2,1)S(1)} %copy-done.8, bf16[2,1024,512]{2,1,0:T(8,128)(2,1)} %param.28), kind=kOutput, calls=%fused_computation.118 | convolution fusion | flops 167772160 | bytes 1507328 | tf_op jit(solution)/shard_map/dot_general | solution.py:121
  21.7 2.5 %fusion.18 = bf16[2048,512]{1,0:T(8,128)(2,1)} fusion(bf16[320,512]{1,0:T(8,128)(2,1)S(1)} %copy-done.8, s32[2048]{0:T(1024)S(1)} %copy-done.18), kind=kOutput, calls=%fused_computation.29 | convolution fusion | flops 672792576 | bytes 2433024 | tf_op jit(solution)/shard_map/dot_general | solution.py:34
  24.3 2.5 %fusion.102 = f32[512,512]{1,0:T(8,128)} fusion(bf16[512,512]{1,0:T(8,128)(2,1)S(1)} %copy-done.7, bf16[2,1536,512]{2,1,0:T(8,128)(2,1)} %param.24), kind=kOutput, calls=%fused_computation.115 | convolution fusion | flops 268435456 | bytes 2097152 | tf_op jit(solution)/shard_map/dot_general | solution.py:39
  27.8 2.4 %copy.19 = bf16[2048,512]{0,1:T(8,128)(2,1)} copy(bf16[2048,512]{1,0:T(8,128)(2,1)S(1)} %copy-done.6) | data formatting | bytes 4194304 | tf_op args[1]
  30.3 1.7 %fusion.16 = bf16[2048,512]{1,0:T(8,128)(2,1)S(1)} fusion(s32[2048]{0:T(1024)S(1)} %copy-done.17, bf16[64,512]{1,0:T(8,128)(2,1)S(1)} %collective-permute-done.1, bf16[320,512]{1,0:T(8,128)(2,1)S(1)} %copy-done.8, bf16[64,512]{1,0:T(8,128)(2,1)S(1)} %collective-permute-done), kind=kOutput, calls=%fused_computation.27 | convolution fusion | flops 942866432 | bytes 2564096 | tf_op jit(solution)/shard_map/dot_general | solution.py:34
  32.0 5.5 %fusion = f32[2048,512]{1,0:T(8,128)} fusion(bf16[2048,512]{1,0:T(8,128)(2,1)S(1)} %copy-done.22, bf16[2048,512]{1,0:T(8,128)(2,1)S(1)} %fusion.16, bf16[2,1536,512]{2,1,0:T(8,128)(2,1)} %param.24), kind=kOutput, calls=%fused_computation | convolution fusion | flops 2155872256 | bytes 9437184 | tf_op jit(solution)/shard_map/dot_general | solution.py:38
  37.5 7.3 %fusion.174 = (f32[2048]{0:T(1024)S(1)}, f32[2048,512]{0,1:T(8,128)}) fusion(bf16[2,512,512]{2,1,0:T(8,128)(2,1)} %param.26, f32[2048,512]{1,0:T(8,128)} %fusion, bf16[2048,512]{1,0:T(8,128)(2,1)S(1)} %copy-done.6, f32[512]{0:T(512)S(1)} %bitcast.118, bf16[2,1536,512]{2,1,0:T(8,128)(2,1)} %param.24), kind=kOutput, calls=%fused_computation.187 | convolution fusion | flops 2155870208 | bytes 11544576 | tf_op jit(solution)/shard_map/dot_general | solution.py:41
  44.8 2.8 %multiply_reduce_fusion.1 = f32[2048]{0:T(1024)S(1)} fusion(f32[2048,512]{0,1:T(8,128)} %get-tuple-element.19, f32[2048]{0:T(1024)S(1)} %broadcast_multiply_fusion.1), kind=kLoop, calls=%fused_computation.17 | loop fusion | flops 3143680 | bytes 4210688 | tf_op jit(solution)/shard_map/reduce_sum | solution.py:29
  48.2 2.0 %fusion.21 = f32[320,512]{1,0:T(8,128)} fusion(f32[2048,512]{0,1:T(8,128)S(1)} %copy-done.1, f32[512]{0:T(512)S(1)} %bitcast.107, f32[2048]{0:T(1024)S(1)} %add_rsqrt_fusion.1, f32[2048]{0:T(1024)S(1)} %broadcast_multiply_fusion.1, s32[2048]{0:T(1024)S(1)} %copy-done.18), kind=kOutput, calls=%fused_computation.33 | convolution fusion | flops 675938304 | bytes 4876288 | tf_op jit(solution)/shard_map/dot_general | solution.py:115
  51.4 3.7 %fusion.42 = bf16[512,512]{1,0:T(8,128)(2,1)} fusion(bf16[2048,512]{1,0:T(8,128)(2,1)} %bitcast.7, s32[512]{0:T(512)S(1)} %add.176), kind=kOutput, calls=%fused_computation.56 | convolution fusion | flops 1075052544 | bytes 2623488 | tf_op jit(solution)/shard_map/dot_general | solution.py:34
  55.1 3.3 %fusion.177 = (f32[512]{0:T(512)S(1)}, f32[512,512]{0,1:T(8,128)S(1)}) fusion(bf16[2,512,512]{2,1,0:T(8,128)(2,1)} %param.26, f32[512,512]{1,0:T(8,128)} %fusion.102, bf16[2,1536,512]{2,1,0:T(8,128)(2,1)} %param.24, bf16[512,512]{1,0:T(8,128)(2,1)} %convolution_convert_fusion.1, bf16[512,512]{1,0:T(8,128)(2,1)} %fusion.42, f32[512]{0:T(512)S(1)} %bitcast.119), kind=kOutput, calls=%fused_computation.188 | convolution fusion | flops 809500160 | bytes 4722688 | tf_op jit(solution)/shard_map/dot_general | solution.py:41
  58.6 3.1 %multiply_convert_fusion.5 = bf16[320,512]{1,0:T(8,128)(2,1)} fusion(f32[320,512]{1,0:T(8,128)} %fusion.106, f32[320,512]{1,0:T(8,128)} %fusion.21, f32[512,512]{0,1:T(8,128)S(1)} %get-tuple-element.21, bf16[2,1024,512]{2,1,0:T(8,128)(2,1)} %param.28, f32[512]{0:T(512)S(1)} %bitcast.109, f32[512]{0:T(512)S(1)} %add_rsqrt_fusion.5, ...), kind=kOutput, calls=%fused_computation.98 | convolution fusion | flops 338231296 | bytes 3221504 | tf_op jit(solution)/shard_map/dot_general | solution.py:122
  61.7 1.6 %fusion.182 = (f32[320]{0:T(512)S(1)}, f32[320,512]{1,0:T(8,128)S(1)}) fusion(bf16[320,512]{1,0:T(8,128)(2,1)} %multiply_convert_fusion.5, bf16[2,512,512]{2,1,0:T(8,128)(2,1)} %param.30), kind=kOutput, calls=%fused_computation.189 | convolution fusion | flops 167935680 | bytes 1508608 | tf_op jit(solution)/shard_map/dot_general | solution.py:126
  63.8 2.3 %fusion.95 = f32[320,512]{1,0:T(8,128)} fusion(bf16[320,512]{1,0:T(8,128)(2,1)S(1)} %add_convert_fusion.5, bf16[2,1024,512]{2,1,0:T(8,128)(2,1)} %param.28), kind=kOutput, calls=%fused_computation.108 | convolution fusion | flops 167772160 | bytes 1507328 | tf_op jit(solution)/shard_map/dot_general | solution.py:121
  66.1 2.5 %fusion.19 = bf16[2048,512]{1,0:T(8,128)(2,1)} fusion(bf16[320,512]{1,0:T(8,128)(2,1)S(1)} %add_convert_fusion.5, s32[2048]{0:T(1024)S(1)} %copy-done.18), kind=kOutput, calls=%fused_computation.30 | convolution fusion | flops 672792576 | bytes 2433024 | tf_op jit(solution)/shard_map/dot_general | solution.py:34
  68.8 2.5 %fusion.91 = f32[512,512]{1,0:T(8,128)} fusion(bf16[512,512]{0,1:T(8,128)(2,1)S(1)} %add_convert_fusion.3, bf16[2,1536,512]{2,1,0:T(8,128)(2,1)} %param.24), kind=kOutput, calls=%fused_computation.105 | convolution fusion | flops 268435456 | bytes 2097152 | tf_op jit(solution)/shard_map/dot_general | solution.py:39
  72.7 3.4 %collective-permute-start.3 = (bf16[64,512]{1,0:T(8,128)(2,1)S(1)}, bf16[64,512]{1,0:T(8,128)(2,1)S(1)}, u32[]{:S(2)}, u32[]{:S(2)}) collective-permute-start(bf16[64,512]{1,0:T(8,128)(2,1)S(1)} %get-tuple-element.7), channel_id=1, source_target_pairs={{1,0},{2,1},{3,2},{4,3},{5,4},{6,5},{7,6},{8,7},{9,8},{10,9},{11,1... | collective-permute-start | bytes 196616 | tf_op jit(solution)/shard_map/ppermute | solution.py:21
  77.4 1.6 %stack.5 = bf16[128,16,512]{2,1,0:T(8,128)(2,1)} broadcast(bf16[16,512]{1,0:T(8,128)(2,1)S(1)} %slice.150), dimensions={1,2} | broadcast | bytes 2113536 | tf_op jit(solution)/shard_map/stack | solution.py:95
  79.0 7.4 %all-to-all-start.1 = ((bf16[128,16,512]{2,1,0:T(8,128)(2,1)}), bf16[128,16,512]{2,1,0:T(8,128)(2,1)}, u32[]{:S(2)}, u32[]{:S(2)}) async-start(bf16[128,16,512]{2,1,0:T(8,128)(2,1)} %stack.5), calls=%async_computation.1 | async-start | bytes 4194304 | tf_op jit(solution)/shard_map/all_to_all | solution.py:94
  88.1 5.6 %fusion.4 = f32[2048,512]{1,0:T(8,128)} fusion(bf16[2048,512]{1,0:T(8,128)(2,1)S(1)} %copy-done.21, bf16[2048,512]{1,0:T(8,128)(2,1)S(1)} %fusion.17, bf16[2,1536,512]{2,1,0:T(8,128)(2,1)} %param.24), kind=kOutput, calls=%fused_computation.4 | convolution fusion | flops 2155872256 | bytes 9437184 | tf_op jit(solution)/shard_map/dot_general | solution.py:38
  93.6 7.3 %fusion.183 = (f32[2048]{0:T(1024)S(1)}, f32[2048,512]{0,1:T(8,128)}) fusion(bf16[2,512,512]{2,1,0:T(8,128)(2,1)} %param.26, f32[2048,512]{1,0:T(8,128)} %fusion.4, bf16[2048,512]{0,1:T(8,128)(2,1)S(1)} %add_convert_fusion.1, f32[512]{0:T(512)S(1)} %bitcast.115, bf16[2,1536,512]{2,1,0:T(8,128)(2,1)} %param.24), kind=kOutput, calls=%fused_computation.190 | convolution fusion | flops 2155870208 | bytes 11544576 | tf_op jit(solution)/shard_map/dot_general | solution.py:41
  101.0 2.8 %multiply_reduce_fusion = f32[2048]{0:T(1024)S(1)} fusion(f32[2048,512]{0,1:T(8,128)} %get-tuple-element.25, f32[2048]{0:T(1024)S(1)} %broadcast_multiply_fusion), kind=kLoop, calls=%fused_computation.10 | loop fusion | flops 3143680 | bytes 4210688 | tf_op jit(solution)/shard_map/reduce_sum | solution.py:29
  104.4 2.5 %add_convert_fusion = bf16[2048,512]{0,1:T(8,128)(2,1)} fusion(bf16[2048,512]{0,1:T(8,128)(2,1)S(1)} %add_convert_fusion.1, f32[2048,512]{0,1:T(8,128)S(1)} %copy-done, f32[512]{0:T(512)S(1)} %bitcast.103, f32[2048]{0:T(1024)S(1)} %add_rsqrt_fusion, f32[2048]{0:T(1024)S(1)} %broadcast_multiply_fusion), kind=kLoop, calls=%fused_computation.8 | loop fusion | flops 6291456 | bytes 8407040 | tf_op jit(solution)/shard_map/convert_element_type | solution.py:43
  106.9 3.9 %copy.21 = bf16[2048,512]{1,0:T(8,128)(2,1)} copy(bf16[2048,512]{0,1:T(8,128)(2,1)} %add_convert_fusion) | data formatting | bytes 4194304
  110.8 4.1 %fusion.20 = f32[320,512]{1,0:T(8,128)} fusion(f32[2048,512]{0,1:T(8,128)} %get-tuple-element.25, f32[512]{0:T(512)S(1)} %bitcast.104, f32[2048]{0:T(1024)S(1)} %add_rsqrt_fusion, f32[2048]{0:T(1024)S(1)} %broadcast_multiply_fusion, s32[2048]{0:T(1024)S(1)} %copy-done.18), kind=kOutput, calls=%fused_computation.32 | convolution fusion | flops 675938304 | bytes 4876288 | tf_op jit(solution)/shard_map/dot_general | solution.py:115
  115.9 3.7 %fusion.43 = bf16[512,512]{1,0:T(8,128)(2,1)} fusion(bf16[2048,512]{1,0:T(8,128)(2,1)} %bitcast.18, s32[512]{0:T(512)S(1)} %add.176), kind=kOutput, calls=%fused_computation.57 | convolution fusion | flops 1075052544 | bytes 2623488 | tf_op jit(solution)/shard_map/dot_general | solution.py:34
  119.6 2.8 %fusion.186 = (f32[512]{0:T(512)S(1)}, f32[512,512]{0,1:T(8,128)S(1)}) fusion(bf16[2,512,512]{2,1,0:T(8,128)(2,1)} %param.26, f32[512,512]{1,0:T(8,128)S(1)} %copy-done.10, bf16[2,1536,512]{2,1,0:T(8,128)(2,1)} %param.24, bf16[512,512]{1,0:T(8,128)(2,1)S(1)} %copy-done.20, bf16[512,512]{1,0:T(8,128)(2,1)} %fusion.43, f32[512]{0:T(512)S(1)} %bitcast.116), kind=kOutput, calls=%fused_computation.191 | convolution fusion | flops 809500160 | bytes 4722688 | tf_op jit(solution)/shard_map/dot_general | solution.py:41
  123.8 2.2 %multiply_convert_fusion.4 = bf16[320,512]{1,0:T(8,128)(2,1)S(1)} fusion(f32[320,512]{1,0:T(8,128)} %fusion.95, f32[320,512]{1,0:T(8,128)} %fusion.20, f32[512,512]{0,1:T(8,128)S(1)} %get-tuple-element.27, bf16[2,1024,512]{2,1,0:T(8,128)(2,1)} %param.28, f32[512]{0:T(512)S(1)} %bitcast.106, f32[512]{0:T(512)S(1)} %add_rsqrt_fusion.3, ...), kind=kOutput, calls=%fused_computation.95 | convolution fusion | flops 338231296 | bytes 3221504 | tf_op jit(solution)/shard_map/dot_general | solution.py:122
  (90 shorter events, 15.6 us)
Async XLA Ops:
  0.6 17.5 %copy-start.8 = (bf16[320,512]{1,0:T(8,128)(2,1)S(1)}, bf16[320,512]{1,0:T(8,128)(2,1)}, u32[]{:S(2)}) copy-start(bf16[320,512]{1,0:T(8,128)(2,1)} %param.16) | copy-start | bytes 983044
  0.6 17.4 %copy-start.11 = (f32[2,512]{1,0:T(2,128)S(1)}, f32[2,512]{1,0:T(2,128)}, u32[]{:S(2)}) copy-start(f32[2,512]{1,0:T(2,128)} %param.25) | copy-start | bytes 12292
  0.7 17.4 %copy-start.12 = (f32[2,512]{1,0:T(2,128)S(1)}, f32[2,512]{1,0:T(2,128)}, u32[]{:S(2)}) copy-start(f32[2,512]{1,0:T(2,128)} %param.27) | copy-start | bytes 12292
  0.7 17.4 %copy-start.13 = (f32[2,512]{1,0:T(2,128)S(1)}, f32[2,512]{1,0:T(2,128)}, u32[]{:S(2)}) copy-start(f32[2,512]{1,0:T(2,128)} %param.29) | copy-start | bytes 12292
  0.7 17.4 %copy-start.14 = (f32[2,512]{1,0:T(2,128)S(1)}, f32[2,512]{1,0:T(2,128)}, u32[]{:S(2)}) copy-start(f32[2,512]{1,0:T(2,128)} %param.31) | copy-start | bytes 12292
  0.7 17.5 %copy-start.19 = (s32[512]{0:T(512)S(1)}, s32[512]{0:T(512)}, u32[]{:S(2)}) copy-start(s32[512]{0:T(512)} %param.23) | copy-start | bytes 6148
  1.7 28.6 %collective-permute-start = (bf16[64,512]{1,0:T(8,128)(2,1)S(1)}, bf16[64,512]{1,0:T(8,128)(2,1)S(1)}, u32[]{:S(2)}, u32[]{:S(2)}) collective-permute-start(bf16[64,512]{1,0:T(8,128)(2,1)S(1)} %get-tuple-element.8), channel_id=1, source_target_pairs={{0,1},{1,2},{2,3},{3,4},{4,5},{5,6},{6,7},{7,8},{8,9},{9,10},{10,1... | collective-permute-start | bytes 196616 | tf_op jit(solution)/shard_map/ppermute | solution.py:18
  3.9 26.4 %collective-permute-start.1 = (bf16[64,512]{1,0:T(8,128)(2,1)S(1)}, bf16[64,512]{1,0:T(8,128)(2,1)S(1)}, u32[]{:S(2)}, u32[]{:S(2)}) collective-permute-start(bf16[64,512]{1,0:T(8,128)(2,1)S(1)} %get-tuple-element.9), channel_id=1, source_target_pairs={{1,0},{2,1},{3,2},{4,3},{5,4},{6,5},{7,6},{8,7},{9,8},{10,9},{11,1... | collective-permute-start | bytes 196616 | tf_op jit(solution)/shard_map/ppermute | solution.py:21
  8.3 13.4 %copy-start.18 = (s32[2048]{0:T(1024)S(1)}, s32[2048]{0:T(1024)}, u32[]{:S(2)}) copy-start(s32[2048]{0:T(1024)} %param.20) | copy-start | bytes 24580
  9.9 41.5 %all-to-all-start = ((bf16[128,16,512]{2,1,0:T(8,128)(2,1)}), bf16[128,16,512]{2,1,0:T(8,128)(2,1)}, u32[]{:S(2)}, u32[]{:S(2)}) async-start(bf16[128,16,512]{2,1,0:T(8,128)(2,1)} %stack.4), calls=%async_computation | async-start | bytes 4194304 | tf_op jit(solution)/shard_map/all_to_all | solution.py:94
  19.4 4.8 %copy-start.7 = (bf16[512,512]{1,0:T(8,128)(2,1)S(1)}, bf16[512,512]{1,0:T(8,128)(2,1)}, u32[]{:S(2)}) copy-start(bf16[512,512]{1,0:T(8,128)(2,1)} %param.18) | copy-start | bytes 1572868
  21.7 5.0 %copy-start.16 = (s32[512,1]{0,1:T(1,128)S(1)}, s32[512,1]{0,1:T(1,128)}, u32[]{:S(2)}) copy-start(s32[512,1]{0,1:T(1,128)} %param.21) | copy-start | bytes 6148
  21.7 6.1 %copy-start.6 = (bf16[2048,512]{1,0:T(8,128)(2,1)S(1)}, bf16[2048,512]{1,0:T(8,128)(2,1)}, u32[]{:S(2)}) copy-start(bf16[2048,512]{1,0:T(8,128)(2,1)} %param.17) | copy-start | bytes 6291460
  24.2 6.0 %copy-start.15 = (s32[512]{0:T(512)S(1)}, s32[512]{0:T(512)}, u32[]{:S(2)}) copy-start(s32[512]{0:T(512)} %param.22) | copy-start | bytes 6148
  24.3 6.0 %copy-start.17 = (s32[2048]{0:T(1024)S(1)}, s32[2048]{0:T(1024)}, u32[]{:S(2)}) copy-start(s32[2048]{0:T(1024)} %param.19) | copy-start | bytes 24580
  30.2 1.8 %copy-start.22 = (bf16[2048,512]{1,0:T(8,128)(2,1)S(1)}, bf16[2048,512]{1,0:T(8,128)(2,1)}, u32[]{:S(2)}) copy-start(bf16[2048,512]{1,0:T(8,128)(2,1)} %fusion.18) | copy-start | bytes 6291460
  44.8 3.4 %copy-start.1 = (f32[2048,512]{0,1:T(8,128)S(1)}, f32[2048,512]{0,1:T(8,128)}, u32[]{:S(2)}) copy-start(f32[2048,512]{0,1:T(8,128)} %get-tuple-element.19) | copy-start | bytes 12582916
  47.6 2.6 %copy-start.2 = (bf16[2048,512]{0,1:T(8,128)(2,1)S(1)}, bf16[2048,512]{0,1:T(8,128)(2,1)}, u32[]{:S(2)}) copy-start(bf16[2048,512]{0,1:T(8,128)(2,1)} %copy.19) | copy-start | bytes 6291460
  58.4 5.2 %copy-start.3 = (f32[512,512]{0,1:T(8,128)}, f32[512,512]{0,1:T(8,128)S(1)}, u32[]{:S(2)}) copy-start(f32[512,512]{0,1:T(8,128)S(1)} %get-tuple-element.21) | copy-start | bytes 3145732
  63.7 4.9 %copy-start.4 = (f32[512,512]{0,1:T(8,128)S(1)}, f32[512,512]{0,1:T(8,128)}, u32[]{:S(2)}) copy-start(f32[512,512]{0,1:T(8,128)} %copy-done.3) | copy-start | bytes 3145732
  63.7 4.9 %copy-start.5 = (bf16[512,512]{0,1:T(8,128)(2,1)S(1)}, bf16[512,512]{0,1:T(8,128)(2,1)}, u32[]{:S(2)}) copy-start(bf16[512,512]{0,1:T(8,128)(2,1)} %copy.20) | copy-start | bytes 1572868
  71.4 15.1 %collective-permute-start.2 = (bf16[64,512]{1,0:T(8,128)(2,1)S(1)}, bf16[64,512]{1,0:T(8,128)(2,1)S(1)}, u32[]{:S(2)}, u32[]{:S(2)}) collective-permute-start(bf16[64,512]{1,0:T(8,128)(2,1)S(1)} %get-tuple-element.6), channel_id=1, source_target_pairs={{0,1},{1,2},{2,3},{3,4},{4,5},{5,6},{6,7},{7,8},{8,9},{9,10},{10,1... | collective-permute-start | bytes 196616 | tf_op jit(solution)/shard_map/ppermute | solution.py:18
  72.7 13.8 %collective-permute-start.3 = (bf16[64,512]{1,0:T(8,128)(2,1)S(1)}, bf16[64,512]{1,0:T(8,128)(2,1)S(1)}, u32[]{:S(2)}, u32[]{:S(2)}) collective-permute-start(bf16[64,512]{1,0:T(8,128)(2,1)S(1)} %get-tuple-element.7), channel_id=1, source_target_pairs={{1,0},{2,1},{3,2},{4,3},{5,4},{6,5},{7,6},{8,7},{9,8},{10,9},{11,1... | collective-permute-start | bytes 196616 | tf_op jit(solution)/shard_map/ppermute | solution.py:21
  79.0 36.8 %all-to-all-start.1 = ((bf16[128,16,512]{2,1,0:T(8,128)(2,1)}), bf16[128,16,512]{2,1,0:T(8,128)(2,1)}, u32[]{:S(2)}, u32[]{:S(2)}) async-start(bf16[128,16,512]{2,1,0:T(8,128)(2,1)} %stack.5), calls=%async_computation.1 | async-start | bytes 4194304 | tf_op jit(solution)/shard_map/all_to_all | solution.py:94
  86.5 1.6 %copy-start.21 = (bf16[2048,512]{1,0:T(8,128)(2,1)S(1)}, bf16[2048,512]{1,0:T(8,128)(2,1)}, u32[]{:S(2)}) copy-start(bf16[2048,512]{1,0:T(8,128)(2,1)} %fusion.19) | copy-start | bytes 6291460
  101.0 3.4 %copy-start = (f32[2048,512]{0,1:T(8,128)S(1)}, f32[2048,512]{0,1:T(8,128)}, u32[]{:S(2)}) copy-start(f32[2048,512]{0,1:T(8,128)} %get-tuple-element.25) | copy-start | bytes 12582916
  114.9 4.6 %copy-start.10 = (f32[512,512]{1,0:T(8,128)S(1)}, f32[512,512]{1,0:T(8,128)}, u32[]{:S(2)}) copy-start(f32[512,512]{1,0:T(8,128)} %fusion.91) | copy-start | bytes 3145732
  114.9 4.6 %copy-start.20 = (bf16[512,512]{1,0:T(8,128)(2,1)S(1)}, bf16[512,512]{1,0:T(8,128)(2,1)}, u32[]{:S(2)}) copy-start(bf16[512,512]{1,0:T(8,128)(2,1)} %convolution_convert_fusion) | copy-start | bytes 1572868
  122.8 3.2 %copy-start.9 = (bf16[2,512,512]{2,1,0:T(8,128)(2,1)S(1)}, bf16[2,512,512]{2,1,0:T(8,128)(2,1)}, u32[]{:S(2)}) copy-start(bf16[2,512,512]{2,1,0:T(8,128)(2,1)} %param.30) | copy-start | bytes 3145732
